TPU v7x, 32 devices: a whole 2x2x4 slice. The times are simulated.
32 devices in a mesh: seq: 8 (over z, core), res: 4 (over y, x).
Axes of the slice: x: 2, y: 2, z: 4, core: 2. Of those that a mesh axis runs over, the one named last changes fastest.
Arguments:
- pair_grad: bfloat16 [32, 512, 128], P('seq', 'res'), may hold values from -128 to 128
- out_weight: bfloat16 [1024, 128], replicated, may hold values from -0.1875 to 0.1875
- left_feat: bfloat16 [32, 32, 1024], P('res', None, 'seq'), may hold values from -6 to 6
- right_feat: bfloat16 [512, 32, 1024], P('res', None, 'seq'), may hold values from -6 to 6
Outputs:
- grad_left: float32 [32, 32, 1024], P('res', None, 'seq')
- grad_right: float32 [512, 32, 1024], P('res', None, 'seq')
All inputs are finite; a program needn't handle non-finite values.
Results may differ from a plain program's by a relative error of at most 0.0029.
Values may be sent and summed in bfloat16 or wider, within the bound.
A program may use at most 64 MiB of HBM per device.

v0:
```python
import math

import jax
import jax.numpy as jnp
from jax import lax
from jax.sharding import PartitionSpec as P

PANEL = 8


def per_device(pair_grad, out_weight, left_feat, right_feat):
    left_all = lax.all_gather(left_feat, "res", axis=0, tiled=True)
    row_count = right_feat.shape[2]
    rows_total = row_count * lax.axis_size("seq")
    n_left = left_all.shape[0]
    width = right_feat.shape[1]
    n_right = right_feat.shape[0]
    initial = (
        jnp.zeros((n_left, width, row_count), jnp.float32),
        jnp.zeros((n_right, width, row_count), jnp.float32),
    )
    carry = initial
    piece = lax.all_gather(pair_grad, "seq", axis=0, tiled=True)
    start = jnp.int32(0)
    count = piece.shape[0]
    stride = math.gcd(count, PANEL)
    for number in range(count // stride):
        sub_rows = piece[number * stride : (number + 1) * stride]
        expand_count = sub_rows.shape[0]
        flat = sub_rows.reshape(expand_count * n_right, sub_rows.shape[2])
        expand_outer = lax.dot_general(
            flat, out_weight, (((1,), (1,)), ((), ())), preferred_element_type=jnp.float32
        )
        outer = expand_outer.astype(jnp.bfloat16).reshape(expand_count, n_right, width * width)
        contract_start = start + number * stride
        contract_count = outer.shape[0]
        four = outer.reshape(contract_count, n_right, width, width)
        left_rows = lax.dynamic_slice_in_dim(left_all, contract_start, contract_count, 0)
        left_part = jnp.einsum(
            "ijce,jes->ics", four, right_feat, preferred_element_type=jnp.float32
        )
        right_part = jnp.einsum(
            "ijce,ics->jes", four, left_rows, preferred_element_type=jnp.float32
        )
        contract_left_acc = lax.dynamic_update_slice_in_dim(carry[0], left_part, contract_start, 0)
        carry = (contract_left_acc, carry[1] + right_part)
    left_acc, right_acc = carry
    inverse = 1.0 / rows_total
    grad_left = lax.psum_scatter(left_acc * inverse, "res", scatter_dimension=0, tiled=True)
    grad_right = right_acc * inverse
    return (grad_left, grad_right)


def solution(mesh):
    in_specs = (P("seq", "res", None), P(), P("res", None, "seq"), P("res", None, "seq"))
    out_specs = (P("res", None, "seq"), P("res", None, "seq"))
    return jax.shard_map(
        per_device, mesh=mesh, in_specs=in_specs, out_specs=out_specs, check_vma=False
    )
```

profile of v0, /device:TPU:0, one launch (start us, length us, event | category | flops | bytes accessed | tf_op | source)
XLA Modules:
  0.0 100.9 jit_solution(1286944372189713724)
XLA Ops:
  7.2 0.7 all-gather.2.cloned.1.call-update
  8.0 10.8 %all_gather.7 = bf16[32,32,128]{2,1,0:T(8,128)(2,1)S(1)} all-gather(bf16[8,32,128]{2,1,0:T(8,128)(2,1)} %param.6), channel_id=1, replica_groups=mesh['seq'=8,'res'=4] {'res'}, dimensions={0}, use_global_device_ids=true | all-gather | bytes 327680 | tf_op jit(solution)/shard_map/all_gather | solution.py:12
  18.7 15.8 %all-gather.2.cloned.1.call-done = bf16[32,128,128]{2,1,0:T(8,128)(2,1)} async-done(((bf16[4,128,128]{2,1,0:T(8,128)(2,1)}), bf16[32,128,128]{2,1,0:T(8,128)(2,1)}) %all-gather.2.cloned.1.call-update) | async-done | bytes 1048592 | tf_op jit(solution)/shard_map/all_gather | solution.py:23
  34.6 1.3 %fusion.15 = (bf16[8,128,128]{2,1,0:T(8,128)(2,1)S(1)}, bf16[8,128,128]{2,1,0:T(8,128)(2,1)S(1)}, bf16[8,128,128]{2,1,0:T(8,128)(2,1)S(1)}, bf16[8,128,128]{2,1,0:T(8,128)(2,1)S(1)}) fusion(bf16[32,128,128]{2,1,0:T(8,128)(2,1)} %all-gather.2.cloned.1.call-done), kind=kLoop, calls=%fused_computation.31 | loop fusion | bytes 2097152 | tf_op jit(solution)/shard_map/slice | solution.py:28
  35.9 0.7 convolution_convert_fusion.3
  36.6 2.6 %copy.36 = bf16[1024,1024]{0,1:T(8,128)(2,1)} copy(bf16[1024,1024]{1,0:T(8,128)(2,1)S(1)} %convolution_convert_fusion.3) | data formatting | bytes 4194304 | tf_op jit(solution)/shard_map/convert_element_type | solution.py:34
  39.1 3.6 %copy.62 = bf16[128,8,8,128]{3,2,1,0:T(8,128)(2,1)} copy(bf16[128,8,8,128]{3,1,2,0:T(8,128)(2,1)} %bitcast.112) | data formatting | bytes 4194304
  42.7 0.7 convolution_convert_fusion.2
  43.4 2.6 %copy.38 = bf16[1024,1024]{0,1:T(8,128)(2,1)} copy(bf16[1024,1024]{1,0:T(8,128)(2,1)S(1)} %convolution_convert_fusion.2) | data formatting | bytes 4194304 | tf_op jit(solution)/shard_map/convert_element_type | solution.py:34
  46.0 3.5 %copy.63 = bf16[128,8,8,128]{3,2,1,0:T(8,128)(2,1)} copy(bf16[128,8,8,128]{3,1,2,0:T(8,128)(2,1)} %bitcast.113) | data formatting | bytes 4194304
  49.5 0.7 convolution_convert_fusion.1
  50.2 2.6 %copy.40 = bf16[1024,1024]{0,1:T(8,128)(2,1)} copy(bf16[1024,1024]{1,0:T(8,128)(2,1)S(1)} %convolution_convert_fusion.1) | data formatting | bytes 4194304 | tf_op jit(solution)/shard_map/convert_element_type | solution.py:34
  52.8 3.5 %copy.64 = bf16[128,8,8,128]{3,2,1,0:T(8,128)(2,1)} copy(bf16[128,8,8,128]{3,1,2,0:T(8,128)(2,1)} %bitcast.114) | data formatting | bytes 4194304
  56.3 0.7 convolution_convert_fusion
  57.0 2.6 %copy.42 = bf16[1024,1024]{0,1:T(8,128)(2,1)} copy(bf16[1024,1024]{1,0:T(8,128)(2,1)S(1)} %convolution_convert_fusion) | data formatting | bytes 4194304 | tf_op jit(solution)/shard_map/convert_element_type | solution.py:34
  59.6 2.4 %copy.65 = bf16[128,8,8,128]{3,2,1,0:T(8,128)(2,1)S(1)} copy(bf16[128,8,8,128]{3,1,2,0:T(8,128)(2,1)} %bitcast.115) | data formatting | bytes 4194304
  62.0 0.1 copy-done.2
  62.2 0.8 convolution_bitcast_fusion.3
  62.9 0.1 dynamic_update_slice.12
  63.0 1.4 %copy-done.3 = bf16[128,8,8,128]{3,2,1,0:T(8,128)(2,1)S(1)} copy-done((bf16[128,8,8,128]{3,2,1,0:T(8,128)(2,1)S(1)}, bf16[128,8,8,128]{3,2,1,0:T(8,128)(2,1)}, u32[]{:S(2)}) %copy-start.3) | copy-done | bytes 2097176
  64.4 0.8 fusion.3
  65.2 0.8 fusion.2
  66.0 0.8 fusion.1
  66.7 0.8 broadcast_multiply_fusion
  67.6 2.7 %fusion.12 = f32[128,32,128,1]{2,0,1,3:T(8,128)S(1)} fusion(bf16[8,128,32,32]{1,0,3,2:T(8,128)(2,1)} %bitcast.110, bf16[8,32,128]{2,1,0:T(8,128)(2,1)S(1)} %get-tuple-element.13), kind=kOutput, calls=%fused_computation.26 | convolution fusion | flops 268435456 | bytes 4259840 | tf_op jit(solution)/shard_map/ijce,ics->jes/dot_general | solution.py:42
  70.3 1.0 fusion.13
  71.3 0.9 fusion.14
  72.3 0.6 copy-done.6
  72.9 1.1 %fusion = f32[128,32,128]{2,0,1:T(8,128)S(1)} fusion(f32[128,32,128,1]{2,0,1,3:T(8,128)S(1)} %fusion.12, f32[128,32,128,1]{2,0,1,3:T(8,128)S(1)} %fusion.13, f32[128,32,128,1]{2,0,1,3:T(8,128)S(1)} %fusion.14, bf16[8,128,32,32]{1,0,3,2:T(8,128)(2,1)S(1)} %bitcast.109, bf16[8,32,128]{2,1,0:T(8,128)(2,1)S(1)} %get-tuple-element.12), kind=kOutput, calls=%fused_computation.1 | convolution fusion | flops 270532608 | bytes 10551296 | tf_op jit(solution)/shard_map/ijce,ics->jes/dot_general | solution.py:42
  74.0 2.5 %copy.49 = f32[128,32,128]{2,1,0:T(8,128)} copy(f32[128,32,128]{2,0,1:T(8,128)S(1)} %fusion) | data formatting | bytes 4194304
  76.5 15.9 %reduce-scatter.2.cloned.1.call-done = f32[8,32,128]{2,0,1:T(8,128)} async-done(((f32[32,32,128]{2,0,1:T(8,128)}), f32[8,32,128]{2,0,1:T(8,128)}) %reduce-scatter.2.cloned.1.call-update) | async-done | bytes 131088 | tf_op jit(solution)/shard_map/reduce_scatter | solution.py:49
  92.4 1.6 %copy.48 = f32[8,32,128]{2,1,0:T(8,128)} copy(f32[8,32,128]{2,0,1:T(8,128)} %reduce-scatter.2.cloned.1.call-done) | data formatting | bytes 262144
  (17 shorter events, 0.1 us)
Async XLA Ops:
  7.2 28.7 %copy-start = (bf16[1024,128]{1,0:T(8,128)(2,1)S(1)}, bf16[1024,128]{1,0:T(8,128)(2,1)}, u32[]{:S(2)}) copy-start(bf16[1024,128]{1,0:T(8,128)(2,1)} %param.5) | copy-start | bytes 786436
  7.2 27.4 %all-gather.2.cloned.1.call-start = ((), (), s32[]{:S(2)}) async-start(), calls=%async_computation.1 | async-start | bytes 1179648 | tf_op jit(solution)/shard_map/all_gather | solution.py:23
  7.9 84.5 %reduce-scatter.2.cloned.1.call-start = ((), (), s32[]{:S(2)}) async-start(), calls=%async_computation.2 | async-start | bytes 655360 | tf_op jit(solution)/shard_map/reduce_scatter | solution.py:49
  59.6 2.4 %copy-start.1 = (bf16[128,32,128]{2,1,0:T(8,128)(2,1)S(1)}, bf16[128,32,128]{2,1,0:T(8,128)(2,1)}, u32[]{:S(2)}) copy-start(bf16[128,32,128]{2,1,0:T(8,128)(2,1)} %param.7) | copy-start | bytes 3145732
  59.6 2.5 %copy-start.2 = (bf16[128,8,8,128]{3,2,1,0:T(8,128)(2,1)S(1)}, bf16[128,8,8,128]{3,2,1,0:T(8,128)(2,1)}, u32[]{:S(2)}) copy-start(bf16[128,8,8,128]{3,2,1,0:T(8,128)(2,1)} %copy.62) | copy-start | bytes 6291460
  62.0 4.0 %copy-start.5 = (bf16[128,8,8,128]{3,2,1,0:T(8,128)(2,1)}, bf16[128,8,8,128]{3,2,1,0:T(8,128)(2,1)S(1)}, u32[]{:S(2)}) copy-start(bf16[128,8,8,128]{3,2,1,0:T(8,128)(2,1)S(1)} %copy.65) | copy-start | bytes 6291460
  62.0 2.4 %copy-start.3 = (bf16[128,8,8,128]{3,2,1,0:T(8,128)(2,1)S(1)}, bf16[128,8,8,128]{3,2,1,0:T(8,128)(2,1)}, u32[]{:S(2)}) copy-start(bf16[128,8,8,128]{3,2,1,0:T(8,128)(2,1)} %copy.63) | copy-start | bytes 6291460
  62.9 2.3 %copy-start.7 = (bf16[128,8,8,128]{3,2,1,0:T(8,128)(2,1)S(1)}, bf16[128,8,8,128]{3,2,1,0:T(8,128)(2,1)}, u32[]{:S(2)}) copy-start(bf16[128,8,8,128]{3,2,1,0:T(8,128)(2,1)} %copy.64) | copy-start | bytes 6291460
  67.6 2.7 %copy-start.4 = (bf16[128,8,8,128]{3,2,1,0:T(8,128)(2,1)S(1)}, bf16[128,8,8,128]{3,2,1,0:T(8,128)(2,1)}, u32[]{:S(2)}) copy-start(bf16[128,8,8,128]{3,2,1,0:T(8,128)(2,1)} %copy.63) | copy-start | bytes 6291460
  71.3 1.6 %copy-start.6 = (bf16[128,8,8,128]{3,2,1,0:T(8,128)(2,1)S(1)}, bf16[128,8,8,128]{3,2,1,0:T(8,128)(2,1)}, u32[]{:S(2)}) copy-start(bf16[128,8,8,128]{3,2,1,0:T(8,128)(2,1)} %copy-done.5) | copy-start | bytes 6291460
Sparse Core Ops, SparseCore 0:
  9.6 24.9 all-gather.1
  67.7 24.6 reduce-scatter.1
where the time goes:
time: 101 us
  waiting for transfers between devices  32.5 us (32%)
  local copies, waits for them, and re-layouts  30.9 us (31%)
  between operations  14.3 us (14%)
  matrix products  11.6 us (11%)
  blocking collectives  10.8 us (11%)
    unnamed x22, local copies, waits for them, and re-layouts  19.3 us
    reduce_scatter x1, waiting for transfers between devices, per_device(): lax.psum_scatter(left_acc * inverse, 'res', scatter_dimension=0, tiled=True)  15.9 us
    all_gather x1, waiting for transfers between devices, per_device(): piece = lax.all_gather(pair_grad, 'seq', axis=0, tiled=True)  15.8 us
    all_gather x1, blocking collectives, per_device(): left_all = lax.all_gather(left_feat, 'res', axis=0, tiled=True)  10.8 us
    convert_element_type x4, local copies, waits for them, and re-layouts, per_device(): expand_outer.astype(jnp.bfloat16)  10.2 us
    dot_general x4, matrix products, per_device(): jnp.einsum('ijce,ics->jes', four, left_rows, preferred_element_type=jnp.f...  5.71 us
    dot_general x4, matrix products, per_device(): jnp.einsum('ijce,jes->ics', four, right_feat, preferred_element_type=jnp....  3.07 us
    dot_general x4, matrix products, per_device(): lax.dot_general(flat, out_weight, (((1,), (1,)), ((), ())), preferred_ele...  2.83 us
  transfers between devices with their start and end apart: 2, of which 2 were waited for; matrix products, arithmetic and copies ran while one was open for 8% of the time, Pallas kernels for 0%

commit v1 on v0

v1 whole, which is shorter than its diff:
```python
import functools
import math

import jax
import jax.numpy as jnp
from jax import lax
from jax.experimental import pallas as pl
from jax.experimental.pallas import tpu as pltpu
from jax.sharding import PartitionSpec as P

MESH = pl.DeviceIdType.MESH
LANES = 128


def kernel(
    sizes, pair_in, weight_in, left_in, right_in, left_out, right_out,
    pair_all, left_all, sum_recv, sum_send, sum_own, raw, wide, right_perm,
    weight_raw, weight_wide, weight_perm, outer, right_acc, left_final,
    local_sem, pair_recv, pair_send, left_recv, left_send, sum_recv_sem, sum_send_sem, out_sem,
):
    n_seq, n_res, i_loc, n_right, width, rows = sizes
    chips = n_seq // 2
    chunk = 2 * i_loc
    n_left = n_seq * i_loc
    owned = n_left // n_res
    piece = math.gcd(chunk, owned)
    inverse = 1.0 / (rows * n_seq)
    q = lax.axis_index("seq")
    r = lax.axis_index("res")
    core = lax.rem(q, 2)
    chip = lax.div(q, 2)
    sibling = chip * 2 + (1 - core)
    lane_blocks = rows // LANES

    block = i_loc * n_right
    share = owned * width

    def pair_slot(source):
        return pair_all.at[pl.ds(pl.multiple_of(source * block, block), block), :]

    def left_slot(source):
        return left_all.at[pl.ds(pl.multiple_of(source * share, share), share), :]

    weight_copy = pltpu.make_async_copy(weight_in, weight_raw, local_sem.at[0])
    weight_copy.start()
    right_copy = pltpu.make_async_copy(right_in, raw, local_sem.at[1])
    right_copy.start()
    left_copy = pltpu.make_async_copy(left_in, left_slot(r), local_sem.at[2])
    left_copy.start()
    pair_copy = pltpu.make_async_copy(pair_in, pair_slot(q), local_sem.at[3])
    pair_copy.start()

    barrier = pltpu.get_barrier_semaphore()

    def greet(seq, res):
        pl.semaphore_signal(
            barrier, inc=1, device_id={"seq": seq, "res": res}, device_id_type=MESH
        )

    has_right = chip < chips - 1
    has_left = chip > 0

    @pl.when(has_right)
    def _():
        greet(q + 2, r)

    @pl.when(has_left)
    def _():
        greet(q - 2, r)

    greet(sibling, r)
    for step in range(1, n_res):
        greet(q, lax.rem(r + step, n_res))

    pl.semaphore_wait(
        barrier, n_res + has_right.astype(jnp.int32) + has_left.astype(jnp.int32)
    )

    def pair_send_to(source_ref, source, way, target):
        return pltpu.make_async_remote_copy(
            src_ref=source_ref, dst_ref=pair_slot(source),
            send_sem=pair_send.at[way, source], recv_sem=pair_recv.at[source],
            device_id={"seq": target, "res": r}, device_id_type=MESH,
        )

    @pl.when(has_right)
    def _():
        pair_send_to(pair_in, q, 0, q + 2).start()

    @pl.when(has_left)
    def _():
        pair_send_to(pair_in, q, 1, q - 2).start()

    pair_send_to(pair_in, q, 2, sibling).start()

    def left_send_to(step):
        return pltpu.make_async_remote_copy(
            src_ref=left_in, dst_ref=left_slot(r),
            send_sem=left_send.at[step], recv_sem=left_recv.at[r],
            device_id={"seq": q, "res": lax.rem(r + step, n_res)}, device_id_type=MESH,
        )

    for step in range(1, n_res):
        left_send_to(step).start()

    weight_copy.wait()
    weight_wide[...] = weight_raw[...].astype(jnp.float32)
    for e in range(width):
        weight_perm[e * width : (e + 1) * width, :] = weight_wide[
            pl.ds(e, width, stride=width), :
        ].astype(jnp.bfloat16)
    right_copy.wait()
    for b in range(lane_blocks):
        lanes = slice(b * LANES, (b + 1) * LANES)
        wide[b] = raw[:, lanes].astype(jnp.float32)
        for e in range(width):
            right_perm[e * n_right : (e + 1) * n_right, lanes] = wide[
                b, pl.ds(e, n_right, stride=width), :
            ].astype(jnp.bfloat16)
    right_acc[...] = jnp.zeros_like(right_acc)

    left_copy.wait()
    pair_copy.wait()
    for step in range(1, n_res):
        source = lax.rem(r + step, n_res)
        pltpu.make_async_copy(left_slot(source), left_slot(source), left_recv.at[source]).wait()

    def pair_wait(source):
        pltpu.make_async_copy(pair_slot(source), pair_slot(source), pair_recv.at[source]).wait()

    def sum_send_to(index, owner):
        offset = lax.rem(index * piece, owned) * width
        return pltpu.make_async_remote_copy(
            src_ref=sum_send.at[pl.ds(pl.multiple_of(index * piece * width, piece * width), piece * width), :],
            dst_ref=sum_recv.at[r, pl.ds(pl.multiple_of(offset, piece * width), piece * width), :],
            send_sem=sum_send_sem.at[index], recv_sem=sum_recv_sem.at[r],
            device_id={"seq": q, "res": owner}, device_id_type=MESH,
        )

    pieces = chunk // piece
    group = max(1, 256 // n_right)
    group = math.gcd(group, chunk)
    span = group * n_right
    columns = width * n_right
    tile = math.gcd(columns, 512)

    def compute(which):
        for p in range(chunk // group):
            start = pl.multiple_of(which * (chunk * n_right) + p * span, span)
            grads = pair_all[pl.ds(start, span), :]
            expanded = lax.dot_general(
                weight_perm[...], grads, (((1,), (1,)), ((), ())), preferred_element_type=jnp.float32
            ).astype(jnp.bfloat16)
            for ii in range(group):
                i = p * group + ii
                for e in range(width):
                    outer[i * width : (i + 1) * width, e * n_right : (e + 1) * n_right] = expanded[
                        e * width : (e + 1) * width, ii * n_right : (ii + 1) * n_right
                    ]
        part = lax.dot_general(
            outer[...], right_perm[...], (((1,), (0,)), ((), ())), preferred_element_type=jnp.float32
        ) * inverse
        first = pl.multiple_of(which * (chunk * width), chunk * width)
        sum_send[pl.ds(first, chunk * width), :] = part.astype(jnp.bfloat16)
        for u in range(pieces):
            index = which * pieces + u
            owner = lax.div(index * piece, owned)

            @pl.when(owner == r)
            def _():
                offset = pl.multiple_of(lax.rem(index * piece, owned) * width, piece * width)
                sum_own[pl.ds(offset, piece * width), :] = part[
                    u * piece * width : (u + 1) * piece * width, :
                ]

            @pl.when(owner != r)
            def _():
                sum_send_to(index, owner).start()

        left_rows = left_all[pl.ds(first, chunk * width), :]
        for t in range(columns // tile):
            at = slice(t * tile, (t + 1) * tile)
            right_acc[:, at] += lax.dot_general(
                left_rows, outer[:, at], (((0,), (0,)), ((), ())), preferred_element_type=jnp.float32
            )

    def ring(d, carry):
        lower = chip - d
        upper = chip + d

        @pl.when((d > 0) & (lower >= 0))
        def _():
            source = lower * 2 + core
            pair_wait(source)

            @pl.when(has_right)
            def _():
                pair_send_to(pair_slot(source), source, 0, q + 2).start()

            pair_send_to(pair_slot(source), source, 2, sibling).start()

        @pl.when((d > 0) & (upper < chips))
        def _():
            source = upper * 2 + core
            pair_wait(source)

            @pl.when(has_left)
            def _():
                pair_send_to(pair_slot(source), source, 1, q - 2).start()

            pair_send_to(pair_slot(source), source, 2, sibling).start()

        def side(s, inner):
            which = chip + (2 * s - 1) * d

            @pl.when((which >= 0) & (which < chips) & ((d > 0) | (s == 0)))
            def _():
                pair_wait(which * 2 + (1 - core))
                compute(which)

            return inner

        return lax.fori_loop(0, 2, side, carry)

    lax.fori_loop(0, chips, ring, 0)

    for b in range(lane_blocks):
        lanes = slice(b * LANES, (b + 1) * LANES)
        for e in range(width):
            wide[b, pl.ds(e, n_right, stride=width), :] = (
                jnp.transpose(right_acc[lanes, e * n_right : (e + 1) * n_right]) * inverse
            )
    right_copies = [
        pltpu.make_async_copy(
            wide.at[b], right_out.at[:, pl.ds(b * LANES, LANES)], out_sem.at[b]
        )
        for b in range(lane_blocks)
    ]
    for copy in right_copies:
        copy.start()

    total = sum_own[...]
    for step in range(1, n_res):
        source = lax.rem(r + step, n_res)
        pltpu.make_async_copy(sum_recv.at[source], sum_recv.at[source], sum_recv_sem.at[source]).wait()
        total = total + sum_recv[source].astype(jnp.float32)
    left_final[...] = total
    final_copy = pltpu.make_async_copy(left_final, left_out, out_sem.at[lane_blocks])
    final_copy.start()

    pair_send_to(pair_in, q, 2, sibling).wait_send()

    @pl.when(has_right)
    def _():
        pair_send_to(pair_in, q, 0, q + 2).wait_send()

    @pl.when(has_left)
    def _():
        pair_send_to(pair_in, q, 1, q - 2).wait_send()

    def settle(d, carry):
        lower = chip - d
        upper = chip + d

        @pl.when(lower >= 0)
        def _():
            source = lower * 2 + core

            @pl.when(has_right)
            def _():
                pair_send_to(pair_slot(source), source, 0, q + 2).wait_send()

            pair_send_to(pair_slot(source), source, 2, sibling).wait_send()

        @pl.when(upper < chips)
        def _():
            source = upper * 2 + core

            @pl.when(has_left)
            def _():
                pair_send_to(pair_slot(source), source, 1, q - 2).wait_send()

            pair_send_to(pair_slot(source), source, 2, sibling).wait_send()

        return carry

    lax.fori_loop(1, chips, settle, 0)
    for step in range(1, n_res):
        left_send_to(step).wait_send()

    def settle_sums(index, carry):
        owner = lax.div(index * piece, owned)

        @pl.when(owner != r)
        def _():
            sum_send_to(index, owner).wait_send()

        return carry

    lax.fori_loop(0, n_left // piece, settle_sums, 0)
    final_copy.wait()
    for copy in right_copies:
        copy.wait()


def per_device(n_seq, n_res, pair_grad, out_weight, left_feat, right_feat):
    i_loc, n_right, pair = pair_grad.shape
    owned, width, rows = left_feat.shape
    n_left = n_seq * i_loc
    chunk = 2 * i_loc
    piece = math.gcd(chunk, owned)
    sizes = (n_seq, n_res, i_loc, n_right, width, rows)
    lane_blocks = rows // LANES
    bf16, f32 = jnp.bfloat16, jnp.float32
    dma = pltpu.SemaphoreType.DMA
    anywhere = pl.BlockSpec(memory_space=pl.ANY)
    grad_left, grad_right = pl.pallas_call(
        functools.partial(kernel, sizes),
        out_shape=(
            jax.ShapeDtypeStruct((owned * width, rows), f32),
            jax.ShapeDtypeStruct((n_right * width, rows), f32),
        ),
        in_specs=[anywhere] * 4,
        out_specs=(anywhere, anywhere),
        scratch_shapes=[
            pltpu.VMEM((n_left * n_right, pair), bf16),
            pltpu.VMEM((n_left * width, rows), bf16),
            pltpu.VMEM((n_res, owned * width, rows), bf16),
            pltpu.VMEM((n_left * width, rows), bf16),
            pltpu.VMEM((owned * width, rows), f32),
            pltpu.VMEM((n_right * width, rows), bf16),
            pltpu.VMEM((lane_blocks, n_right * width, LANES), f32),
            pltpu.VMEM((width * n_right, rows), bf16),
            pltpu.VMEM((width * width, pair), bf16),
            pltpu.VMEM((width * width, pair), f32),
            pltpu.VMEM((width * width, pair), bf16),
            pltpu.VMEM((chunk * width, width * n_right), bf16),
            pltpu.VMEM((rows, width * n_right), f32),
            pltpu.VMEM((owned * width, rows), f32),
            dma((4,)),
            dma((n_seq,)),
            dma((3, n_seq)),
            dma((n_res,)),
            dma((n_res,)),
            dma((n_res,)),
            dma((n_left // piece,)),
            dma((lane_blocks + 1,)),
        ],
        compiler_params=pltpu.CompilerParams(
            collective_id=0, has_side_effects=True, vmem_limit_bytes=48 * 1024 * 1024
        ),
    )(
        pair_grad.reshape(i_loc * n_right, pair),
        out_weight,
        left_feat.reshape(owned * width, rows),
        right_feat.reshape(n_right * width, rows),
    )
    return (
        grad_left.reshape(owned, width, rows),
        grad_right.reshape(n_right, width, rows),
    )


def solution(mesh):
    in_specs = (P("seq", "res", None), P(), P("res", None, "seq"), P("res", None, "seq"))
    out_specs = (P("res", None, "seq"), P("res", None, "seq"))
    body = functools.partial(per_device, mesh.shape["seq"], mesh.shape["res"])
    return jax.shard_map(body, mesh=mesh, in_specs=in_specs, out_specs=out_specs, check_vma=False)
```

time: 101 us -> 33.5 us (0.33)
  the two profiles are of different devices: /device:TPU:0 before, /device:TPU:7 now
where the time goes in v1:
time: 33.5 us; the launch traced here: 33.2 us
  Pallas kernels  26.7 us (80%)
  local copies, waits for them, and re-layouts  5.89 us (18%)
  between operations  0.65 us (2%)
    pallas_call x1, Pallas kernels, per_device(): pl.pallas_call(functools.partial(kernel, sizes), out_shape=(jax.ShapeDtyp...  26.7 us
    unnamed x10, local copies, waits for them, and re-layouts  5.89 us

profile of v1, /device:TPU:7, one launch (start us, length us, event | category | flops | bytes accessed | tf_op | source)
XLA Modules:
  0.0 33.2 jit_solution(14981734782142999970)
XLA Ops:
  0.6 0.0 copy-start
  0.6 1.2 %copy-done = bf16[128,32,128]{2,1,0:T(8,128)(2,1)S(1)} copy-done((bf16[128,32,128]{2,1,0:T(8,128)(2,1)S(1)}, bf16[128,32,128]{2,1,0:T(8,128)(2,1)}, u32[]{:S(2)}) %copy-start) | copy-done | bytes 1048600
  1.9 0.0 copy-start.1
  1.9 0.9 %copy-done.1 = bf16[1024,128]{1,0:T(8,128)(2,1)S(1)} copy-done((bf16[1024,128]{1,0:T(8,128)(2,1)S(1)}, bf16[1024,128]{1,0:T(8,128)(2,1)}, u32[]{:S(2)}) %copy-start.1) | copy-done | bytes 262168
  2.8 0.0 copy-start.2
  2.8 0.9 %copy-done.2 = bf16[4,128,128]{2,1,0:T(8,128)(2,1)S(1)} copy-done((bf16[4,128,128]{2,1,0:T(8,128)(2,1)S(1)}, bf16[4,128,128]{2,1,0:T(8,128)(2,1)}, u32[]{:S(2)}) %copy-start.2) | copy-done | bytes 131096
  3.7 0.0 copy-start.3
  3.7 0.8 %copy-done.3 = bf16[8,32,128]{2,1,0:T(8,128)(2,1)S(1)} copy-done((bf16[8,32,128]{2,1,0:T(8,128)(2,1)S(1)}, bf16[8,32,128]{2,1,0:T(8,128)(2,1)}, u32[]{:S(2)}) %copy-start.3) | copy-done | bytes 65560
  4.6 26.7 %shard_map.59 = (f32[256,128]{1,0:T(8,128)S(1)}, f32[4096,128]{1,0:T(8,128)S(1)}) custom-call(bf16[512,128]{1,0:T(8,128)(2,1)S(1)} %bitcast.7, bf16[1024,128]{1,0:T(8,128)(2,1)S(1)} %copy-done.1, bf16[256,128]{1,0:T(8,128)(2,1)S(1)} %bitcast.9, bf16[4096,128]{1,0:T(8,128)(2,1)S(1)} %bitcast.6), custom_call_target="tpu_custom_call" | custom-call | tf_op jit(solution)/shard_map/pallas_call | solution.py:317
  31.3 0.7 %copy.8 = f32[8,32,128]{2,1,0:T(8,128)} copy(f32[8,32,128]{2,1,0:T(8,128)S(1)} %bitcast.8) | data formatting | bytes 262144
  31.9 1.3 %copy.9 = f32[128,32,128]{2,1,0:T(8,128)} copy(f32[128,32,128]{2,1,0:T(8,128)S(1)} %bitcast.5) | data formatting | bytes 4194304
Async XLA Ops:
  0.6 1.2 %copy-start = (bf16[128,32,128]{2,1,0:T(8,128)(2,1)S(1)}, bf16[128,32,128]{2,1,0:T(8,128)(2,1)}, u32[]{:S(2)}) copy-start(bf16[128,32,128]{2,1,0:T(8,128)(2,1)} %param.7) | copy-start | bytes 3145732
  1.9 0.9 %copy-start.1 = (bf16[1024,128]{1,0:T(8,128)(2,1)S(1)}, bf16[1024,128]{1,0:T(8,128)(2,1)}, u32[]{:S(2)}) copy-start(bf16[1024,128]{1,0:T(8,128)(2,1)} %weight_in.1) | copy-start | bytes 786436
  2.8 0.9 %copy-start.2 = (bf16[4,128,128]{2,1,0:T(8,128)(2,1)S(1)}, bf16[4,128,128]{2,1,0:T(8,128)(2,1)}, u32[]{:S(2)}) copy-start(bf16[4,128,128]{2,1,0:T(8,128)(2,1)} %param.4) | copy-start | bytes 393220
  3.7 0.8 %copy-start.3 = (bf16[8,32,128]{2,1,0:T(8,128)(2,1)S(1)}, bf16[8,32,128]{2,1,0:T(8,128)(2,1)}, u32[]{:S(2)}) copy-start(bf16[8,32,128]{2,1,0:T(8,128)(2,1)} %param.6) | copy-start | bytes 196612

commit v2 on v1

--- a/solution.py
+++ b/solution.py
@@ -15,8 +15,8 @@
 def kernel(
     sizes, pair_in, weight_in, left_in, right_in, left_out, right_out,
     pair_all, left_all, sum_recv, sum_send, sum_own, raw, wide, right_perm,
-    weight_raw, weight_wide, weight_perm, outer, right_acc, left_final,
-    local_sem, pair_recv, pair_send, left_recv, left_send, sum_recv_sem, sum_send_sem, out_sem,
+    weight_raw, weight_wide, weight_perm, outer, right_acc,
+    local_sem, pair_recv, pair_send, left_recv, left_send, sum_recv_sem, sum_send_sem,
 ):
     n_seq, n_res, i_loc, n_right, width, rows = sizes
     chips = n_seq // 2
@@ -227,26 +227,15 @@
     for b in range(lane_blocks):
         lanes = slice(b * LANES, (b + 1) * LANES)
         for e in range(width):
-            wide[b, pl.ds(e, n_right, stride=width), :] = (
+            right_out[b, pl.ds(e, n_right, stride=width), :] = (
                 jnp.transpose(right_acc[lanes, e * n_right : (e + 1) * n_right]) * inverse
             )
-    right_copies = [
-        pltpu.make_async_copy(
-            wide.at[b], right_out.at[:, pl.ds(b * LANES, LANES)], out_sem.at[b]
-        )
-        for b in range(lane_blocks)
-    ]
-    for copy in right_copies:
-        copy.start()
-
     total = sum_own[...]
     for step in range(1, n_res):
         source = lax.rem(r + step, n_res)
         pltpu.make_async_copy(sum_recv.at[source], sum_recv.at[source], sum_recv_sem.at[source]).wait()
         total = total + sum_recv[source].astype(jnp.float32)
-    left_final[...] = total
-    final_copy = pltpu.make_async_copy(left_final, left_out, out_sem.at[lane_blocks])
-    final_copy.start()
+    left_out[...] = total
 
     pair_send_to(pair_in, q, 2, sibling).wait_send()
 
@@ -298,9 +287,6 @@
         return carry
 
     lax.fori_loop(0, n_left // piece, settle_sums, 0)
-    final_copy.wait()
-    for copy in right_copies:
-        copy.wait()
 
 
 def per_device(n_seq, n_res, pair_grad, out_weight, left_feat, right_feat):
@@ -313,15 +299,14 @@
     lane_blocks = rows // LANES
     bf16, f32 = jnp.bfloat16, jnp.float32
     dma = pltpu.SemaphoreType.DMA
-    anywhere = pl.BlockSpec(memory_space=pl.ANY)
     grad_left, grad_right = pl.pallas_call(
         functools.partial(kernel, sizes),
         out_shape=(
             jax.ShapeDtypeStruct((owned * width, rows), f32),
-            jax.ShapeDtypeStruct((n_right * width, rows), f32),
+            jax.ShapeDtypeStruct((lane_blocks, n_right * width, LANES), f32),
         ),
-        in_specs=[anywhere] * 4,
-        out_specs=(anywhere, anywhere),
+        in_specs=[pl.BlockSpec(memory_space=pltpu.HBM)] * 4,
+        out_specs=(pl.BlockSpec(memory_space=pltpu.VMEM),) * 2,
         scratch_shapes=[
             pltpu.VMEM((n_left * n_right, pair), bf16),
             pltpu.VMEM((n_left * width, rows), bf16),
@@ -336,7 +321,6 @@
             pltpu.VMEM((width * width, pair), bf16),
             pltpu.VMEM((chunk * width, width * n_right), bf16),
             pltpu.VMEM((rows, width * n_right), f32),
-            pltpu.VMEM((owned * width, rows), f32),
             dma((4,)),
             dma((n_seq,)),
             dma((3, n_seq)),
@@ -344,20 +328,24 @@
             dma((n_res,)),
             dma((n_res,)),
             dma((n_left // piece,)),
-            dma((lane_blocks + 1,)),
         ],
         compiler_params=pltpu.CompilerParams(
             collective_id=0, has_side_effects=True, vmem_limit_bytes=48 * 1024 * 1024
         ),
     )(
-        pair_grad.reshape(i_loc * n_right, pair),
-        out_weight,
-        left_feat.reshape(owned * width, rows),
-        right_feat.reshape(n_right * width, rows),
+        *(
+            pltpu.with_memory_space_constraint(x, pltpu.HBM)
+            for x in (
+                pair_grad.reshape(i_loc * n_right, pair),
+                out_weight,
+                left_feat.reshape(owned * width, rows),
+                right_feat.reshape(n_right * width, rows),
+            )
+        )
     )
     return (
         grad_left.reshape(owned, width, rows),
-        grad_right.reshape(n_right, width, rows),
+        jnp.moveaxis(grad_right, 0, 1).reshape(n_right, width, rows),
     )
 
 

time: 33.5 us -> 29.2 us (0.87)
  local copies, waits for them, and re-layouts: 5.89 us -> 1.98 us
    unnamed x10 -> x2, local copies, waits for them, and re-layouts: 5.89 us -> 1.98 us
where the time goes in v2:
time: 29.2 us; the launch traced here: 29 us
  Pallas kernels  26.4 us (90%)
  local copies, waits for them, and re-layouts  1.98 us (7%)
  between operations  0.64 us (2%)
    pallas_call x1, Pallas kernels, per_device(): pl.pallas_call(functools.partial(kernel, sizes), out_shape=(jax.ShapeDtyp...  26.4 us
    unnamed x2, local copies, waits for them, and re-layouts  1.98 us

profile of v2, /device:TPU:7, one launch (start us, length us, event | category | flops | bytes accessed | tf_op | source)
XLA Modules:
  0.0 29.0 jit_solution(10399334421386231501)
XLA Ops:
  0.6 26.4 %shard_map.59 = (f32[256,128]{1,0:T(8,128)S(1)}, f32[1,4096,128]{2,1,0:T(8,128)S(1)}) custom-call(bf16[512,128]{1,0:T(8,128)(2,1)} %bitcast.8, bf16[1024,128]{1,0:T(8,128)(2,1)} %weight_in.1, bf16[256,128]{1,0:T(8,128)(2,1)} %bitcast.9, bf16[4096,128]{1,0:T(8,128)(2,1)} %bitcast.7), custom_call_target="tpu_custom_call" | custom-call | tf_op jit(solution)/shard_map/pallas_call | solution.py:302
  27.1 0.7 %copy.8 = f32[8,32,128]{2,1,0:T(8,128)} copy(f32[8,32,128]{2,1,0:T(8,128)S(1)} %bitcast.6) | data formatting | bytes 262144
  27.7 1.3 %copy.9 = f32[128,32,128]{2,1,0:T(8,128)} copy(f32[128,32,128]{2,1,0:T(8,128)S(1)} %bitcast.5) | data formatting | bytes 4194304

commit v3 on v2

--- a/solution.py
+++ b/solution.py
@@ -76,22 +76,58 @@
         barrier, n_res + has_right.astype(jnp.int32) + has_left.astype(jnp.int32)
     )
 
-    def pair_send_to(source_ref, source, way, target):
+    def pair_piece(source, p):
+        start = source * block + p * n_right
+        return pair_all.at[pl.ds(pl.multiple_of(start, n_right), n_right), :]
+
+    def pair_send_to(source_ref, source, p, way, target):
         return pltpu.make_async_remote_copy(
-            src_ref=source_ref, dst_ref=pair_slot(source),
-            send_sem=pair_send.at[way, source], recv_sem=pair_recv.at[source],
+            src_ref=source_ref, dst_ref=pair_piece(source, p),
+            send_sem=pair_send.at[way, source, p], recv_sem=pair_recv.at[source, p],
             device_id={"seq": target, "res": r}, device_id_type=MESH,
         )
 
-    @pl.when(has_right)
-    def _():
-        pair_send_to(pair_in, q, 0, q + 2).start()
-
-    @pl.when(has_left)
-    def _():
-        pair_send_to(pair_in, q, 1, q - 2).start()
-
-    pair_send_to(pair_in, q, 2, sibling).start()
+    def own_sends(act):
+        for p in range(i_loc):
+            own = pair_in.at[pl.ds(p * n_right, n_right), :]
+
+            @pl.when(has_right)
+            def _():
+                act(pair_send_to(own, q, p, 0, q + 2))
+
+            @pl.when(has_left)
+            def _():
+                act(pair_send_to(own, q, p, 1, q - 2))
+
+            act(pair_send_to(own, q, p, 2, sibling))
+
+    def relay(d, p, first, act):
+        lower = chip - d
+        upper = chip + d
+
+        @pl.when(lower >= 0)
+        def _():
+            source = lower * 2 + core
+            first(source, p)
+
+            @pl.when(has_right)
+            def _():
+                act(pair_send_to(pair_piece(source, p), source, p, 0, q + 2))
+
+            act(pair_send_to(pair_piece(source, p), source, p, 2, sibling))
+
+        @pl.when(upper < chips)
+        def _():
+            source = upper * 2 + core
+            first(source, p)
+
+            @pl.when(has_left)
+            def _():
+                act(pair_send_to(pair_piece(source, p), source, p, 1, q - 2))
+
+            act(pair_send_to(pair_piece(source, p), source, p, 2, sibling))
+
+    own_sends(lambda copy: copy.start())
 
     def left_send_to(step):
         return pltpu.make_async_remote_copy(
@@ -119,14 +155,18 @@
             ].astype(jnp.bfloat16)
     right_acc[...] = jnp.zeros_like(right_acc)
 
-    left_copy.wait()
     pair_copy.wait()
-    for step in range(1, n_res):
-        source = lax.rem(r + step, n_res)
-        pltpu.make_async_copy(left_slot(source), left_slot(source), left_recv.at[source]).wait()
-
-    def pair_wait(source):
-        pltpu.make_async_copy(pair_slot(source), pair_slot(source), pair_recv.at[source]).wait()
+
+    def left_wait():
+        left_copy.wait()
+        for step in range(1, n_res):
+            source = lax.rem(r + step, n_res)
+            pltpu.make_async_copy(left_slot(source), left_slot(source), left_recv.at[source]).wait()
+
+    def pair_wait(source, p):
+        pltpu.make_async_copy(
+            pair_piece(source, p), pair_piece(source, p), pair_recv.at[source, p]
+        ).wait()
 
     def sum_send_to(index, owner):
         offset = lax.rem(index * piece, owned) * width
@@ -144,8 +184,10 @@
     columns = width * n_right
     tile = math.gcd(columns, 512)
 
-    def compute(which):
-        for p in range(chunk // group):
+    halves = chunk // group
+
+    def expand(which, s, low, high):
+        for p in range(low, high):
             start = pl.multiple_of(which * (chunk * n_right) + p * span, span)
             grads = pair_all[pl.ds(start, span), :]
             expanded = lax.dot_general(
@@ -154,11 +196,21 @@
             for ii in range(group):
                 i = p * group + ii
                 for e in range(width):
-                    outer[i * width : (i + 1) * width, e * n_right : (e + 1) * n_right] = expanded[
+                    outer[s, i * width : (i + 1) * width, e * n_right : (e + 1) * n_right] = expanded[
                         e * width : (e + 1) * width, ii * n_right : (ii + 1) * n_right
                     ]
+
+    def stage_wait(which, s):
+        for p in range(i_loc):
+            pair_wait(which * 2 + (1 - core), p)
+        expand(which, s, 0, halves // 2)
+
+    def stage_expand(which, s):
+        expand(which, s, halves // 2, halves)
+
+    def stage_left(which, s):
         part = lax.dot_general(
-            outer[...], right_perm[...], (((1,), (0,)), ((), ())), preferred_element_type=jnp.float32
+            outer[s], right_perm[...], (((1,), (0,)), ((), ())), preferred_element_type=jnp.float32
         ) * inverse
         first = pl.multiple_of(which * (chunk * width), chunk * width)
         sum_send[pl.ds(first, chunk * width), :] = part.astype(jnp.bfloat16)
@@ -177,52 +229,38 @@
             def _():
                 sum_send_to(index, owner).start()
 
+    def stage_right(which, s):
+        first = pl.multiple_of(which * (chunk * width), chunk * width)
         left_rows = left_all[pl.ds(first, chunk * width), :]
         for t in range(columns // tile):
             at = slice(t * tile, (t + 1) * tile)
             right_acc[:, at] += lax.dot_general(
-                left_rows, outer[:, at], (((0,), (0,)), ((), ())), preferred_element_type=jnp.float32
+                left_rows, outer[s, :, at], (((0,), (0,)), ((), ())), preferred_element_type=jnp.float32
             )
 
+    stages = [stage_wait, stage_expand, stage_left, stage_right]
+
     def ring(d, carry):
-        lower = chip - d
-        upper = chip + d
-
-        @pl.when((d > 0) & (lower >= 0))
-        def _():
-            source = lower * 2 + core
-            pair_wait(source)
-
-            @pl.when(has_right)
-            def _():
-                pair_send_to(pair_slot(source), source, 0, q + 2).start()
-
-            pair_send_to(pair_slot(source), source, 2, sibling).start()
-
-        @pl.when((d > 0) & (upper < chips))
-        def _():
-            source = upper * 2 + core
-            pair_wait(source)
-
-            @pl.when(has_left)
-            def _():
-                pair_send_to(pair_slot(source), source, 1, q - 2).start()
-
-            pair_send_to(pair_slot(source), source, 2, sibling).start()
-
-        def side(s, inner):
-            which = chip + (2 * s - 1) * d
-
-            @pl.when((which >= 0) & (which < chips) & ((d > 0) | (s == 0)))
-            def _():
-                pair_wait(which * 2 + (1 - core))
-                compute(which)
-
-            return inner
-
-        return lax.fori_loop(0, 2, side, carry)
-
-    lax.fori_loop(0, chips, ring, 0)
+        for p in range(i_loc):
+            relay(d, p, pair_wait, lambda copy: copy.start())
+            if p == i_loc - 1:
+                pl.when(d == 1)(left_wait)
+            todo = stages[p * len(stages) // i_loc : (p + 1) * len(stages) // i_loc]
+
+            def side(s, inner):
+                which = chip + (2 * s - 1) * (d - 1)
+
+                @pl.when((which >= 0) & (which < chips) & ((d > 1) | (s == 0)))
+                def _():
+                    for stage in todo:
+                        stage(which, s)
+
+                return inner
+
+            lax.fori_loop(0, 2, side, 0)
+        return carry
+
+    lax.fori_loop(1, chips + 1, ring, 0)
 
     for b in range(lane_blocks):
         lanes = slice(b * LANES, (b + 1) * LANES)
@@ -237,40 +275,11 @@
         total = total + sum_recv[source].astype(jnp.float32)
     left_out[...] = total
 
-    pair_send_to(pair_in, q, 2, sibling).wait_send()
-
-    @pl.when(has_right)
-    def _():
-        pair_send_to(pair_in, q, 0, q + 2).wait_send()
-
-    @pl.when(has_left)
-    def _():
-        pair_send_to(pair_in, q, 1, q - 2).wait_send()
+    own_sends(lambda copy: copy.wait_send())
 
     def settle(d, carry):
-        lower = chip - d
-        upper = chip + d
-
-        @pl.when(lower >= 0)
-        def _():
-            source = lower * 2 + core
-
-            @pl.when(has_right)
-            def _():
-                pair_send_to(pair_slot(source), source, 0, q + 2).wait_send()
-
-            pair_send_to(pair_slot(source), source, 2, sibling).wait_send()
-
-        @pl.when(upper < chips)
-        def _():
-            source = upper * 2 + core
-
-            @pl.when(has_left)
-            def _():
-                pair_send_to(pair_slot(source), source, 1, q - 2).wait_send()
-
-            pair_send_to(pair_slot(source), source, 2, sibling).wait_send()
-
+        for p in range(i_loc):
+            relay(d, p, lambda source, p: None, lambda copy: copy.wait_send())
         return carry
 
     lax.fori_loop(1, chips, settle, 0)
@@ -319,11 +328,11 @@
             pltpu.VMEM((width * width, pair), bf16),
             pltpu.VMEM((width * width, pair), f32),
             pltpu.VMEM((width * width, pair), bf16),
-            pltpu.VMEM((chunk * width, width * n_right), bf16),
+            pltpu.VMEM((2, chunk * width, width * n_right), bf16),
             pltpu.VMEM((rows, width * n_right), f32),
             dma((4,)),
-            dma((n_seq,)),
-            dma((3, n_seq)),
+            dma((n_seq, i_loc)),
+            dma((3, n_seq, i_loc)),
             dma((n_res,)),
             dma((n_res,)),
             dma((n_res,)),

time: 29.2 us -> 28 us (0.959)
  the two profiles are of different devices: /device:TPU:7 before, /device:TPU:0 now
where the time goes in v3:
time: 28 us; the launch traced here: 27.5 us
  Pallas kernels  24.9 us (89%)
  local copies, waits for them, and re-layouts  1.98 us (7%)
  between operations  0.64 us (2%)
    pallas_call x1, Pallas kernels, per_device(): pl.pallas_call(functools.partial(kernel, sizes), out_shape=(jax.ShapeDtyp...  24.9 us
    unnamed x2, local copies, waits for them, and re-layouts  1.98 us

profile of v3, /device:TPU:0, one launch (start us, length us, event | category | flops | bytes accessed | tf_op | source)
XLA Modules:
  0.0 27.5 jit_solution(16959350700625066873)
XLA Ops:
  0.6 24.9 %shard_map.59 = (f32[256,128]{1,0:T(8,128)S(1)}, f32[1,4096,128]{2,1,0:T(8,128)S(1)}) custom-call(bf16[512,128]{1,0:T(8,128)(2,1)} %bitcast.8, bf16[1024,128]{1,0:T(8,128)(2,1)} %weight_in.1, bf16[256,128]{1,0:T(8,128)(2,1)} %bitcast.9, bf16[4096,128]{1,0:T(8,128)(2,1)} %bitcast.7), custom_call_target="tpu_custom_call" | custom-call | tf_op jit(solution)/shard_map/pallas_call | solution.py:311
  25.6 0.7 %copy.8 = f32[8,32,128]{2,1,0:T(8,128)} copy(f32[8,32,128]{2,1,0:T(8,128)S(1)} %bitcast.6) | data formatting | bytes 262144
  26.2 1.3 %copy.9 = f32[128,32,128]{2,1,0:T(8,128)} copy(f32[128,32,128]{2,1,0:T(8,128)S(1)} %bitcast.5) | data formatting | bytes 4194304

commit v4 on v3

--- a/solution.py
+++ b/solution.py
@@ -10,6 +10,7 @@
 
 MESH = pl.DeviceIdType.MESH
 LANES = 128
+PARTS = 2
 
 
 def kernel(
@@ -20,6 +21,7 @@
 ):
     n_seq, n_res, i_loc, n_right, width, rows = sizes
     chips = n_seq // 2
+    parts = math.gcd(i_loc, PARTS)
     chunk = 2 * i_loc
     n_left = n_seq * i_loc
     owned = n_left // n_res
@@ -76,9 +78,11 @@
         barrier, n_res + has_right.astype(jnp.int32) + has_left.astype(jnp.int32)
     )
 
+    grain = block // parts
+
     def pair_piece(source, p):
-        start = source * block + p * n_right
-        return pair_all.at[pl.ds(pl.multiple_of(start, n_right), n_right), :]
+        start = source * block + p * grain
+        return pair_all.at[pl.ds(pl.multiple_of(start, grain), grain), :]
 
     def pair_send_to(source_ref, source, p, way, target):
         return pltpu.make_async_remote_copy(
@@ -88,8 +92,8 @@
         )
 
     def own_sends(act):
-        for p in range(i_loc):
-            own = pair_in.at[pl.ds(p * n_right, n_right), :]
+        for p in range(parts):
+            own = pair_in.at[pl.ds(p * grain, grain), :]
 
             @pl.when(has_right)
             def _():
@@ -201,7 +205,7 @@
                     ]
 
     def stage_wait(which, s):
-        for p in range(i_loc):
+        for p in range(parts):
             pair_wait(which * 2 + (1 - core), p)
         expand(which, s, 0, halves // 2)
 
@@ -241,11 +245,11 @@
     stages = [stage_wait, stage_expand, stage_left, stage_right]
 
     def ring(d, carry):
-        for p in range(i_loc):
+        for p in range(parts):
             relay(d, p, pair_wait, lambda copy: copy.start())
-            if p == i_loc - 1:
+            if p == parts - 1:
                 pl.when(d == 1)(left_wait)
-            todo = stages[p * len(stages) // i_loc : (p + 1) * len(stages) // i_loc]
+            todo = stages[p * len(stages) // parts : (p + 1) * len(stages) // parts]
 
             def side(s, inner):
                 which = chip + (2 * s - 1) * (d - 1)
@@ -278,7 +282,7 @@
     own_sends(lambda copy: copy.wait_send())
 
     def settle(d, carry):
-        for p in range(i_loc):
+        for p in range(parts):
             relay(d, p, lambda source, p: None, lambda copy: copy.wait_send())
         return carry
 
@@ -304,6 +308,7 @@
     n_left = n_seq * i_loc
     chunk = 2 * i_loc
     piece = math.gcd(chunk, owned)
+    parts = math.gcd(i_loc, PARTS)
     sizes = (n_seq, n_res, i_loc, n_right, width, rows)
     lane_blocks = rows // LANES
     bf16, f32 = jnp.bfloat16, jnp.float32
@@ -331,8 +336,8 @@
             pltpu.VMEM((2, chunk * width, width * n_right), bf16),
             pltpu.VMEM((rows, width * n_right), f32),
             dma((4,)),
-            dma((n_seq, i_loc)),
-            dma((3, n_seq, i_loc)),
+            dma((n_seq, parts)),
+            dma((3, n_seq, parts)),
             dma((n_res,)),
             dma((n_res,)),
             dma((n_res,)),

time: 28 us -> 26.2 us (0.936); the launches traced: 27.5 us -> 26 us
  Pallas kernels: 24.9 us -> 23.4 us
    pallas_call x1, Pallas kernels: 24.9 us -> 23.4 us  [per_device(): pl.pallas_call(functools.partial(kernel, sizes), out_shape=(jax.ShapeDtyp...]
where the time goes in v4:
time: 26.2 us; the launch traced here: 26 us
  Pallas kernels  23.4 us (89%)
  local copies, waits for them, and re-layouts  1.98 us (8%)
  between operations  0.64 us (2%)
    pallas_call x1, Pallas kernels, per_device(): pl.pallas_call(functools.partial(kernel, sizes), out_shape=(jax.ShapeDtyp...  23.4 us
    unnamed x2, local copies, waits for them, and re-layouts  1.98 us

profile of v4, /device:TPU:0, one launch (start us, length us, event | category | flops | bytes accessed | tf_op | source)
XLA Modules:
  0.0 26.0 jit_solution(1543449820521841272)
XLA Ops:
  0.6 23.4 %shard_map.59 = (f32[256,128]{1,0:T(8,128)S(1)}, f32[1,4096,128]{2,1,0:T(8,128)S(1)}) custom-call(bf16[512,128]{1,0:T(8,128)(2,1)} %bitcast.8, bf16[1024,128]{1,0:T(8,128)(2,1)} %weight_in.1, bf16[256,128]{1,0:T(8,128)(2,1)} %bitcast.9, bf16[4096,128]{1,0:T(8,128)(2,1)} %bitcast.7), custom_call_target="tpu_custom_call" | custom-call | tf_op jit(solution)/shard_map/pallas_call | solution.py:316
  24.0 0.7 %copy.8 = f32[8,32,128]{2,1,0:T(8,128)} copy(f32[8,32,128]{2,1,0:T(8,128)S(1)} %bitcast.6) | data formatting | bytes 262144
  24.7 1.3 %copy.9 = f32[128,32,128]{2,1,0:T(8,128)} copy(f32[128,32,128]{2,1,0:T(8,128)S(1)} %bitcast.5) | data formatting | bytes 4194304

commit v5 on v4

--- a/solution.py
+++ b/solution.py
@@ -249,7 +249,7 @@
             relay(d, p, pair_wait, lambda copy: copy.start())
             if p == parts - 1:
                 pl.when(d == 1)(left_wait)
-            todo = stages[p * len(stages) // parts : (p + 1) * len(stages) // parts]
+            todo = stages if p == parts - 1 else []
 
             def side(s, inner):
                 which = chip + (2 * s - 1) * (d - 1)

time: 26.2 us -> 25.7 us (0.981)
  Pallas kernels: 23.4 us -> 22.9 us
    pallas_call x1, Pallas kernels: 23.4 us -> 22.9 us  [per_device(): pl.pallas_call(functools.partial(kernel, sizes), out_shape=(jax.ShapeDtyp...]
where the time goes in v5:
time: 25.7 us; the launch traced here: 25.5 us
  Pallas kernels  22.9 us (89%)
  local copies, waits for them, and re-layouts  1.98 us (8%)
  between operations  0.64 us (2%)
    pallas_call x1, Pallas kernels, per_device(): pl.pallas_call(functools.partial(kernel, sizes), out_shape=(jax.ShapeDtyp...  22.9 us
    unnamed x2, local copies, waits for them, and re-layouts  1.98 us

profile of v5, /device:TPU:0, one launch (start us, length us, event | category | flops | bytes accessed | tf_op | source)
XLA Modules:
  0.0 25.5 jit_solution(4620505076636605802)
XLA Ops:
  0.6 22.9 %shard_map.59 = (f32[256,128]{1,0:T(8,128)S(1)}, f32[1,4096,128]{2,1,0:T(8,128)S(1)}) custom-call(bf16[512,128]{1,0:T(8,128)(2,1)} %bitcast.8, bf16[1024,128]{1,0:T(8,128)(2,1)} %weight_in.1, bf16[256,128]{1,0:T(8,128)(2,1)} %bitcast.9, bf16[4096,128]{1,0:T(8,128)(2,1)} %bitcast.7), custom_call_target="tpu_custom_call" | custom-call | tf_op jit(solution)/shard_map/pallas_call | solution.py:316
  23.6 0.7 %copy.8 = f32[8,32,128]{2,1,0:T(8,128)} copy(f32[8,32,128]{2,1,0:T(8,128)S(1)} %bitcast.6) | data formatting | bytes 262144
  24.2 1.3 %copy.9 = f32[128,32,128]{2,1,0:T(8,128)} copy(f32[128,32,128]{2,1,0:T(8,128)S(1)} %bitcast.5) | data formatting | bytes 4194304
